TPU v7x, 128 devices: a whole 4x4x4 slice. The times are simulated.
128 devices in a mesh: pipe: 16 (over x_hi, z, core), tensor: 4 (over y), dp: 2 (over x_lo).
Axes of the slice: x: 4 (x_hi: 2, x_lo: 2; x = x_hi * 2 + x_lo), y: 4, z: 4, core: 2. Of those that a mesh axis runs over, the one named last changes fastest.
Arguments:
- query_heads: bfloat16 [32, 512, 4096], P(('dp', 'pipe'), None, 'tensor'), parts along dimension 0, may hold values from -5 to 5, as said below
- key_heads: bfloat16 [32, 512, 4096], P(('dp', 'pipe'), None, 'tensor'), parts along dimension 0, may hold values from -5 to 5
- value_heads: bfloat16 [32, 512, 4096], P(('dp', 'pipe'), None, 'tensor'), parts along dimension 0, may hold values from -16 to 16
- segment_ids: int32 [32, 512], P(('dp', 'pipe')), parts along dimension 0, may hold values from 0 to 3, never falling along the last dimension, each value on 1 to 256 neighbouring positions
- section_input: bfloat16 [32, 512, 8192], P(('dp', 'pipe'), 'tensor'), parts along dimension 0, may hold values from -6 to 6
- out_weight: bfloat16 [32, 4096, 8192], P(('dp', 'pipe'), 'tensor'), parts along dimension 0, may hold values from -0.1875 to 0.1875
Outputs:
- received: bfloat16 [32, 512, 8192], P(('dp', 'pipe'), 'tensor'), parts along dimension 0
- evicted: bfloat16 [32, 512, 8192], P(('dp', 'pipe'), 'tensor'), parts along dimension 0
- evicted_scale: float32 [32, 512], P(('dp', 'pipe'), 'tensor'), parts along dimension 0
There are 2 independent parts, one for each index of `dp`. A program takes and returns all parts, laid end to end along the dimension named above; each array names one. Nothing has to cross between parts.
Inputs may be any that keep to these rules, and one draw needn't show every extreme that they name: `query_heads`: queries and keys are bfloat16 values of moderate size. `segment_ids`: each section's segment numbers never fall along the tokens; every document is 1 to 256 tokens long.
All inputs are finite; a program needn't handle non-finite values. Where the computation divides by a largest or mean magnitude, that divisor is 1e-20 or more.
Results may differ from a plain program's by a relative error of at most 0.0055.
Values may be sent and summed in bfloat16 or wider, within the bound.
A program may use at most 128 MiB of HBM per device.

v0:
```python
import math

import jax
import jax.numpy as jnp
from jax import lax
from jax.sharding import PartitionSpec as P

HD = 128


def shifted(value, axis, steps):
    count = lax.axis_size(axis)
    leading, last = (max(0, -steps), min(count, count - steps))
    return lax.ppermute(value, axis, [(source, source + steps) for source in range(leading, last)])


def from_partner(value, axis, apart):
    mask = 2**apart
    pairs = [(source, source ^ mask) for source in range(lax.axis_size(axis))]
    return lax.ppermute(value, axis, pairs)


def per_device(query_heads, key_heads, value_heads, segment_ids, section_input, out_weight):
    query_block = query_heads[0]
    key_block = key_heads[0]
    value_block = value_heads[0]
    segment_row = segment_ids[0]
    input_block = section_input[0]
    weight_block = out_weight[0]
    row_count = query_block.shape[0]
    head_count = query_block.shape[1] // HD
    query_three = query_block.reshape(row_count, head_count, HD)
    key_three = key_block.reshape(row_count, head_count, HD)
    value_three = value_block.reshape(row_count, head_count, HD)
    position = jnp.arange(row_count, dtype=jnp.int32)
    allowed = (segment_row[:, None] == segment_row[None, :]) & (
        position[None, :] <= position[:, None]
    )
    scores = jnp.einsum(
        "qhd,khd->hqk", query_three, key_three, preferred_element_type=jnp.float32
    ) * (1.0 / math.sqrt(HD))
    scores = jnp.where(allowed[None, :, :], scores, jnp.float32(-1e30))
    row_max = jnp.max(scores, axis=2, keepdims=True)
    expons = jnp.exp(scores - row_max)
    weights = (expons / jnp.sum(expons, axis=2, keepdims=True)).astype(jnp.bfloat16)
    heads_out = jnp.einsum("hqk,khd->qhd", weights, value_three, preferred_element_type=jnp.float32)
    heads_out = heads_out.astype(jnp.bfloat16).reshape(row_count, head_count * HD)
    wide_input = input_block.astype(jnp.float32)
    scale = jnp.max(jnp.abs(wide_input), axis=1) + 1e-06
    packed = (wide_input / scale[:, None]).astype(jnp.bfloat16)
    partial_value = jnp.dot(heads_out, weight_block, preferred_element_type=jnp.float32)
    mine = lax.psum_scatter(partial_value, "tensor", scatter_dimension=0, tiled=True)
    section_out = (wide_input + mine).astype(jnp.bfloat16)
    received = shifted(section_out[None], "pipe", 1)
    bit_total = lax.axis_size("pipe").bit_length() - 1
    moving = (packed[None], scale[None])
    for bit_index in range(bit_total):
        moving = (
            from_partner(moving[0], "pipe", bit_index),
            from_partner(moving[1].astype(jnp.bfloat16), "pipe", bit_index).astype(jnp.float32),
        )
    evicted, evicted_scale = moving
    return (received, evicted, evicted_scale)


def solution(mesh):
    return jax.shard_map(
        per_device,
        mesh=mesh,
        in_specs=(
            P(("dp", "pipe"), None, "tensor"),
            P(("dp", "pipe"), None, "tensor"),
            P(("dp", "pipe"), None, "tensor"),
            P(("dp", "pipe"), None),
            P(("dp", "pipe"), "tensor", None),
            P(("dp", "pipe"), "tensor", None),
        ),
        out_specs=(
            P(("dp", "pipe"), "tensor", None),
            P(("dp", "pipe"), "tensor", None),
            P(("dp", "pipe"), "tensor"),
        ),
        check_vma=False,
    )
```

profile of v0, /device:TPU:6, one launch (start us, length us, event | category | flops | bytes accessed | tf_op | source)
XLA Modules:
  0.0 372.0 jit_solution(15267259977894930063)
XLA Ops:
  7.2 0.0 reduce-scatter.2.cloned.1.call-start
  7.2 1.0 fusion.18
  8.2 1.5 copy.15
  9.7 1.5 copy.16
  11.2 2.3 copy.14
  13.5 1.3 fusion.15
  14.7 0.0 copy-start.1
  14.7 0.0 slice-start
  14.7 0.0 slice-start.1
  14.8 5.7 %fusion.21 = (f32[8,512]{1,0:T(8,128)S(1)}, f32[8,512,512]{1,2,0:T(8,128)}) fusion(f32[8,512,512]{1,2,0:T(8,128)S(1)} %fusion.15, pred[512,512]{0,1:T(8,128)(4,1)S(1)} %fusion.18), kind=kOutput, calls=%fused_computation.29 | output fusion | flops 12583423 | bytes 17055744 | tf_op jit(solution)/shard_map/sub | solution.py:44
  20.4 0.0 copy-done.1
  20.5 0.0 slice-start.2
  20.5 0.0 slice-start.3
  20.5 4.3 %fusion.14 = bf16[8,512,128]{1,2,0:T(8,128)(2,1)S(1)} fusion(bf16[512,8,128]{0,2,1:T(8,128)(2,1)S(1)} %bitcast.39, f32[8,512,512]{1,2,0:T(8,128)} %get-tuple-element.8, f32[8,512]{1,0:T(8,128)S(1)} %get-tuple-element.7), kind=kOutput, calls=%fused_computation.19 | convolution fusion | flops 541589504 | bytes 10502144 | tf_op jit(solution)/shard_map/hqk,khd->qhd/dot_general | solution.py:46
  24.7 0.0 slice-done
  24.7 0.0 slice-done.1
  24.7 0.3 slice-done.2
  25.1 1.2 slice-done.3
  26.3 11.7 %fusion.1 = f32[512,8192]{1,0:T(8,128)} fusion(bf16[512,1024]{0,1:T(8,128)(2,1)S(1)} %bitcast.34, bf16[1,1024,8192]{2,1,0:T(8,128)(2,1)S(1)} %bitcast.33), kind=kOutput, calls=%fused_computation.1 | convolution fusion | flops 8589934592 | bytes 34603008 | tf_op jit(solution)/shard_map/dot_general | solution.py:51
  37.9 0.0 copy-start
  37.9 0.0 reduce-scatter.2.cloned.1.call-update
  38.0 150.4 %reduce-scatter.2.cloned.1.call-done = f32[128,8192]{1,0:T(8,128)} async-done(((f32[512,8192]{1,0:T(8,128)}), f32[128,8192]{1,0:T(8,128)}) %reduce-scatter.2.cloned.1.call-update) | async-done | bytes 4194320 | tf_op jit(solution)/shard_map/reduce_scatter | solution.py:52
  188.4 0.0 copy-done
  188.4 2.9 fusion.7
  191.3 0.5 fusion.8
  191.8 0.1 collective-permute-start.1
  191.9 4.1 %collective-permute-done.1 = bf16[1,128,8192]{2,1,0:T(8,128)(2,1)S(1)} collective-permute-done((bf16[1,128,8192]{2,1,0:T(8,128)(2,1)S(1)}, bf16[1,128,8192]{2,1,0:T(8,128)(2,1)S(1)}, u32[]{:S(2)}, u32[]{:S(2)}) %collective-permute-start.1) | collective-permute-done | bytes 2097184 | tf_op jit(solution)/shard_map/ppermute | solution.py:20
  196.1 1.6 collective-permute-start.2
  197.6 46.1 %collective-permute-done.2 = bf16[1,128,8192]{2,1,0:T(8,128)(2,1)S(1)} collective-permute-done((bf16[1,128,8192]{2,1,0:T(8,128)(2,1)S(1)}, bf16[1,128,8192]{2,1,0:T(8,128)(2,1)S(1)}, u32[]{:S(2)}, u32[]{:S(2)}) %collective-permute-start.2) | collective-permute-done | bytes 2097184 | tf_op jit(solution)/shard_map/ppermute | solution.py:20
  243.7 3.2 collective-permute-start.3
  246.9 1.9 collective-permute-start
  248.8 67.4 %collective-permute-done.3 = bf16[1,128,8192]{2,1,0:T(8,128)(2,1)S(1)} collective-permute-done((bf16[1,128,8192]{2,1,0:T(8,128)(2,1)S(1)}, bf16[1,128,8192]{2,1,0:T(8,128)(2,1)S(1)}, u32[]{:S(2)}, u32[]{:S(2)}) %collective-permute-start.3) | collective-permute-done | bytes 2097184 | tf_op jit(solution)/shard_map/ppermute | solution.py:20
  316.2 0.0 collective-permute-start.4
  316.2 0.0 collective-permute-start.5
  316.2 1.2 collective-permute-done.5
  317.3 0.0 collective-permute-start.6
  317.3 3.6 collective-permute-done.6
  320.9 0.0 collective-permute-start.7
  320.9 5.1 %collective-permute-done.7 = bf16[1,128]{1,0:T(2,128)(2,1)S(1)} collective-permute-done((bf16[1,128]{1,0:T(2,128)(2,1)S(1)}, bf16[1,128]{1,0:T(2,128)(2,1)S(1)}, u32[]{:S(2)}, u32[]{:S(2)}) %collective-permute-start.7) | collective-permute-done | bytes 288 | tf_op jit(solution)/shard_map/ppermute | solution.py:20
  326.0 3.5 collective-permute-start.8
  329.5 32.5 %collective-permute-done.8 = bf16[1,128]{1,0:T(2,128)(2,1)S(1)} collective-permute-done((bf16[1,128]{1,0:T(2,128)(2,1)S(1)}, bf16[1,128]{1,0:T(2,128)(2,1)S(1)}, u32[]{:S(2)}, u32[]{:S(2)}) %collective-permute-start.8) | collective-permute-done | bytes 288 | tf_op jit(solution)/shard_map/ppermute | solution.py:20
  362.0 0.5 convert_element_type.58
  362.5 0.0 collective-permute-done
  362.5 0.0 collective-permute-done.4
  362.5 1.3 copy.23
  363.9 1.3 copy.24
  (2 shorter events, 0.0 us)
Async XLA Ops:
  7.2 181.2 %reduce-scatter.2.cloned.1.call-start = ((), (), s32[]{:S(2)}) async-start(), calls=%async_computation.1 | async-start | bytes 20971520 | tf_op jit(solution)/shard_map/reduce_scatter | solution.py:52
  14.7 5.7 %copy-start.1 = (bf16[1,512,1024]{1,2,0:T(8,128)(2,1)S(1)}, bf16[1,512,1024]{1,2,0:T(8,128)(2,1)}, u32[]{:S(2)}) copy-start(bf16[1,512,1024]{1,2,0:T(8,128)(2,1)} %copy.14) | copy-start | bytes 3145732
  14.7 10.0 %slice-start = ((s8[16777216]{0:T(1024)(128)(4,1)}), s8[4194304]{0:T(1024)(128)(4,1)S(1)}, s32[]{:S(2)}) async-start(s8[16777216]{0:T(1024)(128)(4,1)} %bitcast.32), calls=%async_computation.2 | async-start | bytes 8388608
  14.7 10.0 %slice-start.1 = ((s8[16777216]{0:T(1024)(128)(4,1)}), s8[4194304]{0:T(1024)(128)(4,1)S(1)}, s32[]{:S(2)}) async-start(s8[16777216]{0:T(1024)(128)(4,1)} %bitcast.32), calls=%async_computation.3 | async-start | bytes 8388608
  20.5 4.6 %slice-start.2 = ((s8[16777216]{0:T(1024)(128)(4,1)}), s8[4194304]{0:T(1024)(128)(4,1)S(1)}, s32[]{:S(2)}) async-start(s8[16777216]{0:T(1024)(128)(4,1)} %bitcast.32), calls=%async_computation.4 | async-start | bytes 8388608
  20.5 5.8 %slice-start.3 = ((s8[16777216]{0:T(1024)(128)(4,1)}), s8[4194304]{0:T(1024)(128)(4,1)S(1)}, s32[]{:S(2)}) async-start(s8[16777216]{0:T(1024)(128)(4,1)} %bitcast.32), calls=%async_computation.5 | async-start | bytes 8388608
  37.9 150.5 %copy-start = (bf16[1,128,8192]{2,1,0:T(8,128)(2,1)S(1)}, bf16[1,128,8192]{2,1,0:T(8,128)(2,1)}, u32[]{:S(2)}) copy-start(bf16[1,128,8192]{2,1,0:T(8,128)(2,1)} %param.10) | copy-start | bytes 6291460
  191.8 4.2 %collective-permute-start.1 = (bf16[1,128,8192]{2,1,0:T(8,128)(2,1)S(1)}, bf16[1,128,8192]{2,1,0:T(8,128)(2,1)S(1)}, u32[]{:S(2)}, u32[]{:S(2)}) collective-permute-start(bf16[1,128,8192]{2,1,0:T(8,128)(2,1)S(1)} %fusion.8), channel_id=1, source_target_pairs={{0,8},{8,0},{16,24},{24,16},{32,40},{40,32},{48,56},{56,48},{64,72... | collective-permute-start | bytes 6291464 | tf_op jit(solution)/shard_map/ppermute | solution.py:20
  196.1 47.7 %collective-permute-start.2 = (bf16[1,128,8192]{2,1,0:T(8,128)(2,1)S(1)}, bf16[1,128,8192]{2,1,0:T(8,128)(2,1)S(1)}, u32[]{:S(2)}, u32[]{:S(2)}) collective-permute-start(bf16[1,128,8192]{2,1,0:T(8,128)(2,1)S(1)} %collective-permute-done.1), channel_id=1, source_target_pairs={{0,16},{8,24},{16,0},{24,8},{32,48},{40,56},{48,32},{56,40},{64,80... | collective-permute-start | bytes 6291464 | tf_op jit(solution)/shard_map/ppermute | solution.py:20
  243.7 72.4 %collective-permute-start.3 = (bf16[1,128,8192]{2,1,0:T(8,128)(2,1)S(1)}, bf16[1,128,8192]{2,1,0:T(8,128)(2,1)S(1)}, u32[]{:S(2)}, u32[]{:S(2)}) collective-permute-start(bf16[1,128,8192]{2,1,0:T(8,128)(2,1)S(1)} %collective-permute-done.2), channel_id=1, source_target_pairs={{0,32},{8,40},{16,48},{24,56},{32,0},{40,8},{48,16},{56,24},{64,96... | collective-permute-start | bytes 6291464 | tf_op jit(solution)/shard_map/ppermute | solution.py:20
  246.9 115.7 %collective-permute-start = (bf16[1,128,8192]{2,1,0:T(8,128)(2,1)S(1)}, bf16[1,128,8192]{2,1,0:T(8,128)(2,1)S(1)}, u32[]{:S(2)}, u32[]{:S(2)}) collective-permute-start(bf16[1,128,8192]{2,1,0:T(8,128)(2,1)S(1)} %get-tuple-element.4), channel_id=1, source_target_pairs={{0,8},{8,16},{16,24},{24,32},{32,40},{40,48},{48,56},{56,64},{64,7... | collective-permute-start | bytes 6291464 | tf_op jit(solution)/shard_map/ppermute | solution.py:14
  316.2 46.4 %collective-permute-start.4 = (bf16[1,128,8192]{2,1,0:T(8,128)(2,1)S(1)}, bf16[1,128,8192]{2,1,0:T(8,128)(2,1)S(1)}, u32[]{:S(2)}, u32[]{:S(2)}) collective-permute-start(bf16[1,128,8192]{2,1,0:T(8,128)(2,1)S(1)} %collective-permute-done.3), channel_id=1, source_target_pairs={{0,64},{8,72},{16,80},{24,88},{32,96},{40,104},{48,112},{56,120},{... | collective-permute-start | bytes 6291464 | tf_op jit(solution)/shard_map/ppermute | solution.py:20
  316.2 1.2 collective-permute-start.5
  317.3 3.6 collective-permute-start.6
  320.9 5.1 %collective-permute-start.7 = (bf16[1,128]{1,0:T(2,128)(2,1)S(1)}, bf16[1,128]{1,0:T(2,128)(2,1)S(1)}, u32[]{:S(2)}, u32[]{:S(2)}) collective-permute-start(bf16[1,128]{1,0:T(2,128)(2,1)S(1)} %collective-permute-done.6), channel_id=1, source_target_pairs={{0,32},{8,40},{16,48},{24,56},{32,0},{40,8},{48,16},{56,24},{64,96... | collective-permute-start | bytes 776 | tf_op jit(solution)/shard_map/ppermute | solution.py:20
  326.0 36.1 %collective-permute-start.8 = (bf16[1,128]{1,0:T(2,128)(2,1)S(1)}, bf16[1,128]{1,0:T(2,128)(2,1)S(1)}, u32[]{:S(2)}, u32[]{:S(2)}) collective-permute-start(bf16[1,128]{1,0:T(2,128)(2,1)S(1)} %collective-permute-done.7), channel_id=1, source_target_pairs={{0,64},{8,72},{16,80},{24,88},{32,96},{40,104},{48,112},{56,120},{... | collective-permute-start | bytes 776 | tf_op jit(solution)/shard_map/ppermute | solution.py:20
Sparse Core Ops, SparseCore 0:
  38.1 150.2 reduce-scatter.1
where the time goes:
time: 372 us
  waiting for transfers between devices  310 us (83%)
  matrix products  17.2 us (5%)
  between operations  14.1 us (4%)
  other arithmetic  10.6 us (3%)
  starting transfers between devices  10.3 us (3%)
  local copies, waits for them, and re-layouts  9.45 us (3%)
    ppermute x8, waiting for transfers between devices, from_partner(): return lax.ppermute(value, axis, pairs)  160 us
    reduce_scatter x1, waiting for transfers between devices, per_device(): lax.psum_scatter(partial_value, 'tensor', scatter_dimension=0, tiled=True)  150 us
    dot_general x1, matrix products, per_device(): jnp.dot(heads_out, weight_block, preferred_element_type=jnp.float32)  11.7 us
    ppermute x8, starting transfers between devices, from_partner(): return lax.ppermute(value, axis, pairs)  8.32 us
  transfers between devices with their start and end apart: 10, of which 8 were waited for; matrix products, arithmetic and copies ran while one was open for 0% of the time, Pallas kernels for 0%

commit v1 on v0

v1 whole, which is shorter than its diff:
```python
import functools
import math

import jax
import jax.numpy as jnp
from jax import lax
from jax.experimental import pallas as pl
from jax.experimental.pallas import tpu as pltpu
from jax.sharding import PartitionSpec as P

HD = 128
NEG = -1e30
MESH = pl.DeviceIdType.MESH


def kernel(
    dims,
    q_hbm, k_hbm, v_hbm, seg_ref, x_hbm, w_hbm,
    recv_hbm, ev_hbm, es_ref,
    q_v, k_v, v_v, x_v, w_v, heads, bias, part, send0, ring, ev_v, scale_v, zero_v,
    in_sem, w_sem, rs_send, rs_recv, fw_send, fw_recv, ev_send, ev_recv, ev_out_sem, zero_sem,
):
    sections, parts, rows, head_count, blocks, width, ev_blocks, ev_rows = dims
    total_rows = parts * rows
    p = lax.axis_index("pipe")
    y = lax.axis_index("tensor")
    d = lax.axis_index("dp")
    up = (p, lax.rem(y + 1, parts), d)
    down = (p, lax.rem(y + parts - 1, parts), d)
    ring_to = (up, down)
    mirror = (sections - 1 - p, y, d)
    after = (lax.rem(p + 1, sections), y, d)
    before = (lax.rem(p + sections - 1, sections), y, d)

    barrier = pltpu.get_barrier_semaphore()
    for device in (up, down, mirror, before):
        pl.semaphore_signal(barrier, inc=1, device_id=device, device_id_type=MESH)

    loads = []
    for i, (src, dst) in enumerate(((q_hbm, q_v), (k_hbm, k_v), (v_hbm, v_v))):
        copy = pltpu.make_async_copy(src.at[0], dst, in_sem.at[i])
        copy.start()
        loads.append(copy)

    def w_copy(side, j):
        cols = pl.ds(pl.multiple_of((side * blocks + j) * width, width), width)
        return pltpu.make_async_copy(w_hbm.at[0, :, cols], w_v.at[side, j], w_sem.at[side, j])

    def start_w(j, carry):
        w_copy(0, j).start()
        w_copy(1, j).start()
        return carry

    lax.fori_loop(0, blocks, start_w, 0)
    x_load = pltpu.make_async_copy(x_hbm.at[0], x_v, in_sem.at[3])
    x_load.start()

    chunk = (
        lax.rem(y + parts - 1, parts),
        lax.rem(y + 2, parts),
        y,
        lax.rem(y + 1, parts),
    )

    def attend(slot):
        start = pl.multiple_of(chunk[slot] * rows, rows)
        seg_all = seg_ref[...].astype(jnp.float32)
        seg_rows = seg_ref[:, pl.ds(start, rows)].astype(jnp.float32)
        seg_col = jnp.broadcast_to(seg_rows, (rows, rows)).T[:, :1]
        row_pos = lax.broadcasted_iota(jnp.int32, (rows, total_rows), 0) + start
        col_pos = lax.broadcasted_iota(jnp.int32, (rows, total_rows), 1)
        allowed = (seg_col == seg_all) & (col_pos <= row_pos)
        bias[...] = jnp.where(allowed, 0.0, NEG)

        def one_head(h, carry):
            cols = pl.ds(pl.multiple_of(h * HD, HD), HD)
            scores = lax.dot_general(
                q_v[pl.ds(start, rows), cols], k_v[:, cols],
                (((1,), (1,)), ((), ())), preferred_element_type=jnp.float32,
            )
            scores = scores * (math.log2(math.e) / math.sqrt(HD)) + bias[...]
            expons = jnp.exp2(scores - jnp.max(scores, axis=1, keepdims=True))
            inverse = 1.0 / jnp.sum(expons, axis=1, keepdims=True)
            weights = (expons * inverse).astype(jnp.bfloat16)
            out = jnp.dot(weights, v_v[:, cols], preferred_element_type=jnp.float32)
            heads[slot * rows:(slot + 1) * rows, cols] = out.astype(jnp.bfloat16)
            return carry

        lax.fori_loop(0, head_count, one_head, 0)

    def ring_copy(side, step, j):
        src = send0.at[side, j] if step == 0 else ring.at[side, step - 1, j]
        return pltpu.make_async_remote_copy(
            src_ref=src, dst_ref=ring.at[side, step, j],
            send_sem=rs_send.at[side, step, j], recv_sem=rs_recv.at[side, step, j],
            device_id=ring_to[side], device_id_type=MESH,
        )

    def first(side, j):
        slot = 0 if side == 0 else 3
        w_copy(side, j).wait()
        out = jnp.dot(
            heads[slot * rows:(slot + 1) * rows, :], w_v[side, j],
            preferred_element_type=jnp.float32,
        )
        send0[side, j] = out.astype(jnp.bfloat16)
        ring_copy(side, 0, j).start()

    def ev_copy(i):
        at = pl.ds(pl.multiple_of(i * ev_rows, ev_rows), ev_rows)
        return pltpu.make_async_remote_copy(
            src_ref=x_hbm.at[0, at, :], dst_ref=ev_v.at[i],
            send_sem=ev_send.at[i], recv_sem=ev_recv.at[i],
            device_id=mirror, device_id_type=MESH,
        )

    def ev_store(i):
        at = pl.ds(pl.multiple_of(i * ev_rows, ev_rows), ev_rows)
        return pltpu.make_async_copy(ev_v.at[i], ev_hbm.at[0, at, :], ev_out_sem.at[i])

    for copy in loads:
        copy.wait()
    attend(0)
    pl.semaphore_wait(barrier, 4)

    lead = 2

    def lead_step(j, carry):
        first(0, j)
        return carry

    lax.fori_loop(0, lead, lead_step, 0)

    def start_ev(i, carry):
        ev_copy(i).start()
        return carry

    lax.fori_loop(0, ev_blocks, start_ev, 0)
    attend(3)

    def first_step(j, carry):
        first(1, j)

        @pl.when(j + lead < blocks)
        def _():
            first(0, j + lead)

        return carry

    lax.fori_loop(0, blocks, first_step, 0)
    attend(1)
    attend(2)

    lo = ((0, 2 * rows, rows), (rows, 0, 2 * rows))

    def add_step(side, step, j):
        ring_copy(side, step, j).wait_recv()
        at = lo[side][step]
        total = ring[side, step, j].astype(jnp.float32) + part[side, j, at:at + rows, :]
        if step == 2:
            cols = pl.ds(pl.multiple_of((side * blocks + j) * width, width), width)
            total = total + x_v[:, cols].astype(jnp.float32)
        ring[side, step, j] = total.astype(jnp.bfloat16)

    def second_step(j, carry):
        for side in (0, 1):
            src = heads[rows:, :] if side == 0 else heads[:3 * rows, :]
            part[side, j] = jnp.dot(src, w_v[side, j], preferred_element_type=jnp.float32)
        for side in (0, 1):
            add_step(side, 0, j)
            ring_copy(side, 1, j).start()
        return carry

    lax.fori_loop(0, blocks, second_step, 0)

    def third_step(j, carry):
        for side in (0, 1):
            add_step(side, 1, j)
            ring_copy(side, 2, j).start()
        return carry

    lax.fori_loop(0, blocks, third_step, 0)
    x_load.wait()

    def out_cols(side, j):
        return pl.ds(pl.multiple_of((side * blocks + j) * width, width), width)

    def fw_copy(side, j):
        return pltpu.make_async_remote_copy(
            src_ref=ring.at[side, 2, j], dst_ref=recv_hbm.at[0, :, out_cols(side, j)],
            send_sem=fw_send.at[side, j], recv_sem=fw_recv.at[side, j],
            device_id=after, device_id_type=MESH,
        )

    def zero_copy(side, j):
        return pltpu.make_async_copy(zero_v, recv_hbm.at[0, :, out_cols(side, j)], zero_sem.at[side, j])

    @pl.when(p == 0)
    def _():
        zero_v[...] = jnp.zeros_like(zero_v)

        def start_zero(j, carry):
            for side in (0, 1):
                zero_copy(side, j).start()
            return carry

        lax.fori_loop(0, blocks, start_zero, 0)

    def evict(i):
        ev_copy(i).wait_recv()
        wide = ev_v[i].astype(jnp.float32)
        scale = jnp.max(jnp.abs(wide), axis=1, keepdims=True) + 1e-06
        ev_v[i] = (wide / scale).astype(jnp.bfloat16)
        at = pl.ds(pl.multiple_of(i * ev_rows, ev_rows), ev_rows)
        scale_v[at, :] = jnp.broadcast_to(scale, (ev_rows, HD))
        ev_store(i).start()

    def last_step(j, carry):
        for side in (0, 1):
            add_step(side, 2, j)

            @pl.when(p < sections - 1)
            def _():
                fw_copy(side, j).start()

        @pl.when(2 * j < ev_blocks)
        def _():
            evict(2 * j)
            evict(2 * j + 1)

        return carry

    lax.fori_loop(0, blocks, last_step, 0)
    es_ref[...] = scale_v[...].T[:1, :]

    def drain(j, carry):
        for side in (0, 1):
            for step in range(3):
                ring_copy(side, step, j).wait_send()

            @pl.when(p < sections - 1)
            def _():
                fw_copy(side, j).wait_send()

            @pl.when(p > 0)
            def _():
                fw_copy(side, j).wait_recv()

            @pl.when(p == 0)
            def _():
                zero_copy(side, j).wait()

        return carry

    lax.fori_loop(0, blocks, drain, 0)

    def drain_ev(i, carry):
        ev_copy(i).wait_send()
        ev_store(i).wait()
        return carry

    lax.fori_loop(0, ev_blocks, drain_ev, 0)


def solution(mesh):
    sections, parts = mesh.shape["pipe"], mesh.shape["tensor"]

    def per_device(query_heads, key_heads, value_heads, segment_ids, section_input, out_weight):
        total_rows, inner = query_heads.shape[1:]
        rows, features = section_input.shape[1:]
        blocks = 8
        width = features // (2 * blocks)
        ev_blocks = 8
        ev_rows = rows // ev_blocks
        dims = (sections, parts, rows, inner // HD, blocks, width, ev_blocks, ev_rows)
        bf16, f32 = jnp.bfloat16, jnp.float32
        any_spec = pl.BlockSpec(memory_space=pl.ANY)
        vmem_spec = pl.BlockSpec(memory_space=pltpu.VMEM)
        dma = pltpu.SemaphoreType.DMA
        return pl.pallas_call(
            functools.partial(kernel, dims),
            out_shape=(
                jax.ShapeDtypeStruct((1, rows, features), bf16),
                jax.ShapeDtypeStruct((1, rows, features), bf16),
                jax.ShapeDtypeStruct((1, rows), f32),
            ),
            in_specs=[any_spec, any_spec, any_spec, vmem_spec, any_spec, any_spec],
            out_specs=(any_spec, any_spec, vmem_spec),
            scratch_shapes=[
                pltpu.VMEM((total_rows, inner), bf16),
                pltpu.VMEM((total_rows, inner), bf16),
                pltpu.VMEM((total_rows, inner), bf16),
                pltpu.VMEM((rows, features), bf16),
                pltpu.VMEM((2, blocks, inner, width), bf16),
                pltpu.VMEM((total_rows, inner), bf16),
                pltpu.VMEM((rows, total_rows), f32),
                pltpu.VMEM((2, blocks, 3 * rows, width), f32),
                pltpu.VMEM((2, blocks, rows, width), bf16),
                pltpu.VMEM((2, 3, blocks, rows, width), bf16),
                pltpu.VMEM((ev_blocks, ev_rows, features), bf16),
                pltpu.VMEM((rows, HD), f32),
                pltpu.VMEM((rows, width), bf16),
                dma((4,)),
                dma((2, blocks)),
                dma((2, 3, blocks)),
                dma((2, 3, blocks)),
                dma((2, blocks)),
                dma((2, blocks)),
                dma((ev_blocks,)),
                dma((ev_blocks,)),
                dma((ev_blocks,)),
                dma((2, blocks)),
            ],
            compiler_params=pltpu.CompilerParams(
                collective_id=0, has_side_effects=True, vmem_limit_bytes=60 * 1024 * 1024
            ),
        )(query_heads, key_heads, value_heads, segment_ids, section_input, out_weight)

    return jax.shard_map(
        per_device,
        mesh=mesh,
        in_specs=(
            P(("dp", "pipe"), None, "tensor"),
            P(("dp", "pipe"), None, "tensor"),
            P(("dp", "pipe"), None, "tensor"),
            P(("dp", "pipe"), None),
            P(("dp", "pipe"), "tensor", None),
            P(("dp", "pipe"), "tensor", None),
        ),
        out_specs=(
            P(("dp", "pipe"), "tensor", None),
            P(("dp", "pipe"), "tensor", None),
            P(("dp", "pipe"), "tensor"),
        ),
        check_vma=False,
    )
```

time: 372 us -> 96.4 us (0.26)
  waiting for transfers between devices: 310 us -> 0 us
  Pallas kernels: 0 us -> 90.5 us
  matrix products: 17.2 us -> 0 us
  between operations: 14.1 us -> 0.65 us
  other arithmetic: 10.6 us -> 0 us
  starting transfers between devices: 10.3 us -> 0 us
  local copies, waits for them, and re-layouts: 9.45 us -> 5.08 us
    ppermute x9 -> x0, waiting for transfers between devices: 160 us -> none  [the longest x8 160 us: from_partner(): return lax.ppermute(value, axis, pairs)]
    reduce_scatter x1 -> x0, waiting for transfers between devices: 150 us -> none  [per_device(): lax.psum_scatter(partial_value, 'tensor', scatter_dimension=0, tiled=True)]
    pallas_call x0 -> x1, Pallas kernels: none -> 90.5 us  [per_device(): pl.pallas_call(functools.partial(kernel, dims), out_shape=(jax.ShapeDtype...]
    dot_general x3 -> x0, matrix products: 17.2 us -> none  [the longest x1 11.7 us: per_device(): jnp.dot(heads_out, weight_block, preferred_element_type=jnp.float32)]
    ppermute x9 -> x0, starting transfers between devices: 10.2 us -> none  [the longest x8 8.32 us: from_partner(): return lax.ppermute(value, axis, pairs)]
    sub x1 -> x0, other arithmetic: 5.69 us -> none  [per_device(): expons = jnp.exp(scores - row_max)]
  transfers between devices with their start and end apart: 10 -> 0, of which waited for: 8 -> 0; matrix products, arithmetic and copies ran while one was open for 0% -> 0% of each run, Pallas kernels for 0% -> 0%
where the time goes in v1:
time: 96.4 us; the launch traced here: 96.3 us
  Pallas kernels  90.5 us (94%)
  local copies, waits for them, and re-layouts  5.08 us (5%)
    pallas_call x1, Pallas kernels, per_device(): pl.pallas_call(functools.partial(kernel, dims), out_shape=(jax.ShapeDtype...  90.5 us
    unnamed x7, local copies, waits for them, and re-layouts  5.08 us

profile of v1, /device:TPU:6, one launch (start us, length us, event | category | flops | bytes accessed | tf_op | source)
XLA Modules:
  0.0 96.3 jit_solution(12809500477854833768)
XLA Ops:
  0.6 90.5 %shard_map.85 = (bf16[1,128,8192]{2,1,0:T(8,128)(2,1)}, bf16[1,128,8192]{2,1,0:T(8,128)(2,1)}, f32[1,128]{1,0:T(1,128)}) custom-call(bf16[1,512,1024]{2,1,0:T(8,128)(2,1)} %q_hbm.1, bf16[1,512,1024]{2,1,0:T(8,128)(2,1)} %k_hbm.1, bf16[1,512,1024]{2,1,0:T(8,128)(2,1)} %v_hbm.1, s32[1,512]{1,0:T(1,128)} %seg_ref.1, bf16[1,128,8192]{2,1,0:T(8,128)(2,1)} %x_hbm.1, ...), custom_call_target="tpu_custom_call" | custom-call | tf_op jit(solution)/shard_map/pallas_call | solution.py:280
  91.2 0.0 copy-start
  91.2 3.2 %copy.12 = bf16[1,128,8192]{2,1,0:T(8,128)(2,1)} copy(bf16[1,128,8192]{2,1,0:T(8,128)(2,1)} %get-tuple-element.6) | data formatting | bytes 4194304
  94.4 0.0 copy-done
  94.4 0.0 copy-start.1
  94.4 1.3 %copy.13 = bf16[1,128,8192]{2,1,0:T(8,128)(2,1)} copy(bf16[1,128,8192]{2,1,0:T(8,128)(2,1)S(1)} %copy-done) | data formatting | bytes 4194304
  95.8 0.0 copy-done.1
  95.8 0.5 copy.14
Async XLA Ops:
  91.2 3.3 %copy-start = (bf16[1,128,8192]{2,1,0:T(8,128)(2,1)S(1)}, bf16[1,128,8192]{2,1,0:T(8,128)(2,1)}, u32[]{:S(2)}) copy-start(bf16[1,128,8192]{2,1,0:T(8,128)(2,1)} %get-tuple-element.7) | copy-start | bytes 6291460
  94.4 1.3 %copy-start.1 = (f32[1,128]{1,0:T(1,128)S(1)}, f32[1,128]{1,0:T(1,128)}, u32[]{:S(2)}) copy-start(f32[1,128]{1,0:T(1,128)} %get-tuple-element.8) | copy-start | bytes 1540

commit v2 on v1

--- a/solution.py
+++ b/solution.py
@@ -11,13 +11,14 @@
 HD = 128
 NEG = -1e30
 MESH = pl.DeviceIdType.MESH
+UNROLL = 4
 
 
 def kernel(
     dims,
     q_hbm, k_hbm, v_hbm, seg_ref, x_hbm, w_hbm,
-    recv_hbm, ev_hbm, es_ref,
-    q_v, k_v, v_v, x_v, w_v, heads, bias, part, send0, ring, ev_v, scale_v, zero_v,
+    recv_out, ev_out, es_ref,
+    q_v, k_v, v_v, x_v, w_v, heads, seg_t, bias, part, send0, ring, ev_v, scale_v, zero_v,
     in_sem, w_sem, rs_send, rs_recv, fw_send, fw_recv, ev_send, ev_recv, ev_out_sem, zero_sem,
 ):
     sections, parts, rows, head_count, blocks, width, ev_blocks, ev_rows = dims
@@ -36,57 +37,80 @@
     for device in (up, down, mirror, before):
         pl.semaphore_signal(barrier, inc=1, device_id=device, device_id_type=MESH)
 
-    loads = []
-    for i, (src, dst) in enumerate(((q_hbm, q_v), (k_hbm, k_v), (v_hbm, v_v))):
-        copy = pltpu.make_async_copy(src.at[0], dst, in_sem.at[i])
-        copy.start()
-        loads.append(copy)
-
-    def w_copy(side, j):
-        cols = pl.ds(pl.multiple_of((side * blocks + j) * width, width), width)
-        return pltpu.make_async_copy(w_hbm.at[0, :, cols], w_v.at[side, j], w_sem.at[side, j])
-
-    def start_w(j, carry):
-        w_copy(0, j).start()
-        w_copy(1, j).start()
-        return carry
-
-    lax.fori_loop(0, blocks, start_w, 0)
-    x_load = pltpu.make_async_copy(x_hbm.at[0], x_v, in_sem.at[3])
-    x_load.start()
-
     chunk = (
         lax.rem(y + parts - 1, parts),
         lax.rem(y + 2, parts),
         y,
         lax.rem(y + 1, parts),
     )
-
-    def attend(slot):
-        start = pl.multiple_of(chunk[slot] * rows, rows)
-        seg_all = seg_ref[...].astype(jnp.float32)
-        seg_rows = seg_ref[:, pl.ds(start, rows)].astype(jnp.float32)
-        seg_col = jnp.broadcast_to(seg_rows, (rows, rows)).T[:, :1]
-        row_pos = lax.broadcasted_iota(jnp.int32, (rows, total_rows), 0) + start
-        col_pos = lax.broadcasted_iota(jnp.int32, (rows, total_rows), 1)
-        allowed = (seg_col == seg_all) & (col_pos <= row_pos)
-        bias[...] = jnp.where(allowed, 0.0, NEG)
-
-        def one_head(h, carry):
-            cols = pl.ds(pl.multiple_of(h * HD, HD), HD)
-            scores = lax.dot_general(
-                q_v[pl.ds(start, rows), cols], k_v[:, cols],
-                (((1,), (1,)), ((), ())), preferred_element_type=jnp.float32,
-            )
-            scores = scores * (math.log2(math.e) / math.sqrt(HD)) + bias[...]
-            expons = jnp.exp2(scores - jnp.max(scores, axis=1, keepdims=True))
-            inverse = 1.0 / jnp.sum(expons, axis=1, keepdims=True)
-            weights = (expons * inverse).astype(jnp.bfloat16)
-            out = jnp.dot(weights, v_v[:, cols], preferred_element_type=jnp.float32)
-            heads[slot * rows:(slot + 1) * rows, cols] = out.astype(jnp.bfloat16)
+    pairs = ((0, 3), (1, 2))
+    group = head_count // 2
+
+    def rows_at(slot):
+        return pl.multiple_of(chunk[slot] * rows, rows)
+
+    def q_copy(pair, i):
+        slot = pairs[pair][i]
+        return pltpu.make_async_copy(
+            q_hbm.at[0, pl.ds(rows_at(slot), rows), :],
+            q_v.at[pair, pl.ds(i * rows, rows), :],
+            in_sem.at[2 * pair + i],
+        )
+
+    def kv_copy(i, part_of):
+        src, dst = ((k_hbm, k_v), (v_hbm, v_v))[i]
+        cols = pl.ds(part_of * group * HD, group * HD)
+        return pltpu.make_async_copy(
+            src.at[0, :, cols], dst.at[:, cols], in_sem.at[4 + 2 * part_of + i]
+        )
+
+    x_load = pltpu.make_async_copy(x_hbm.at[0], x_v, in_sem.at[8])
+
+    def w_copy(side, j):
+        cols = pl.ds(pl.multiple_of((side * blocks + j) * width, width), width)
+        return pltpu.make_async_copy(w_hbm.at[0, :, cols], w_v.at[side, j], w_sem.at[side, j])
+
+    for i in (0, 1):
+        q_copy(0, i).start()
+    for part_of in (0, 1):
+        for i in (0, 1):
+            kv_copy(i, part_of).start()
+
+    seg_all = seg_ref[...].astype(jnp.float32)
+    seg_t[...] = jnp.broadcast_to(seg_all, (rows, total_rows)).T
+
+    def set_bias(pair):
+        for i in (0, 1):
+            start = rows_at(pairs[pair][i])
+            seg_rows = seg_ref[:, pl.ds(start, rows)].astype(jnp.float32)
+            key_pos = lax.broadcasted_iota(jnp.int32, (total_rows, rows), 0)
+            row_pos = lax.broadcasted_iota(jnp.int32, (total_rows, rows), 1) + start
+            allowed = (seg_t[...] == seg_rows) & (key_pos <= row_pos)
+            bias[:, i * rows:(i + 1) * rows] = jnp.where(allowed, 0.0, NEG)
+
+    def attend(pair, first_head, count):
+        def some_heads(i, carry):
+            for u in range(UNROLL):
+                h = first_head + i * UNROLL + u
+                cols = pl.ds(pl.multiple_of(h * HD, HD), HD)
+                scores = lax.dot_general(
+                    k_v[:, cols], q_v[pair, :, cols],
+                    (((1,), (1,)), ((), ())), preferred_element_type=jnp.float32,
+                )
+                scores = scores * (math.log2(math.e) / math.sqrt(HD)) + bias[...]
+                expons = jnp.exp2(scores - jnp.max(scores, axis=0, keepdims=True))
+                inverse = 1.0 / jnp.sum(expons, axis=0, keepdims=True)
+                weights = (expons * inverse).astype(jnp.bfloat16)
+                out = lax.dot_general(
+                    weights, v_v[:, cols],
+                    (((0,), (0,)), ((), ())), preferred_element_type=jnp.float32,
+                ).astype(jnp.bfloat16)
+                for i_slot in (0, 1):
+                    at = pairs[pair][i_slot] * rows
+                    heads[at:at + rows, cols] = out[i_slot * rows:(i_slot + 1) * rows]
             return carry
 
-        lax.fori_loop(0, head_count, one_head, 0)
+        lax.fori_loop(0, count // UNROLL, some_heads, 0)
 
     def ring_copy(side, step, j):
         src = send0.at[side, j] if step == 0 else ring.at[side, step - 1, j]
@@ -116,40 +140,42 @@
 
     def ev_store(i):
         at = pl.ds(pl.multiple_of(i * ev_rows, ev_rows), ev_rows)
-        return pltpu.make_async_copy(ev_v.at[i], ev_hbm.at[0, at, :], ev_out_sem.at[i])
-
-    for copy in loads:
-        copy.wait()
-    attend(0)
+        return pltpu.make_async_copy(ev_v.at[i], ev_out.at[0, at, :], ev_out_sem.at[i])
+
+    def start_w(j, carry):
+        w_copy(0, j).start()
+        w_copy(1, j).start()
+        return carry
+
+    set_bias(0)
+    for i in (0, 1):
+        q_copy(0, i).wait()
+        kv_copy(i, 0).wait()
+    attend(0, 0, group)
+    for i in (0, 1):
+        kv_copy(i, 1).wait()
+    lax.fori_loop(0, blocks, start_w, 0)
+    for i in (0, 1):
+        q_copy(1, i).start()
+    x_load.start()
+    attend(0, group, group)
     pl.semaphore_wait(barrier, 4)
 
-    lead = 2
-
-    def lead_step(j, carry):
+    def first_step(j, carry):
         first(0, j)
-        return carry
-
-    lax.fori_loop(0, lead, lead_step, 0)
-
-    def start_ev(i, carry):
-        ev_copy(i).start()
-        return carry
-
-    lax.fori_loop(0, ev_blocks, start_ev, 0)
-    attend(3)
-
-    def first_step(j, carry):
         first(1, j)
 
-        @pl.when(j + lead < blocks)
+        @pl.when(j < ev_blocks)
         def _():
-            first(0, j + lead)
+            ev_copy(j).start()
 
         return carry
 
     lax.fori_loop(0, blocks, first_step, 0)
-    attend(1)
-    attend(2)
+    set_bias(1)
+    for i in (0, 1):
+        q_copy(1, i).wait()
+    attend(1, 0, head_count)
 
     lo = ((0, 2 * rows, rows), (rows, 0, 2 * rows))
 
@@ -187,13 +213,13 @@
 
     def fw_copy(side, j):
         return pltpu.make_async_remote_copy(
-            src_ref=ring.at[side, 2, j], dst_ref=recv_hbm.at[0, :, out_cols(side, j)],
+            src_ref=ring.at[side, 2, j], dst_ref=recv_out.at[0, :, out_cols(side, j)],
             send_sem=fw_send.at[side, j], recv_sem=fw_recv.at[side, j],
             device_id=after, device_id_type=MESH,
         )
 
     def zero_copy(side, j):
-        return pltpu.make_async_copy(zero_v, recv_hbm.at[0, :, out_cols(side, j)], zero_sem.at[side, j])
+        return pltpu.make_async_copy(zero_v, recv_out.at[0, :, out_cols(side, j)], zero_sem.at[side, j])
 
     @pl.when(p == 0)
     def _():
@@ -262,12 +288,24 @@
     lax.fori_loop(0, ev_blocks, drain_ev, 0)
 
 
+def finish(*refs):
+    srcs, dsts, sems = refs[:3], refs[3:6], refs[6]
+    copies = [
+        pltpu.make_async_copy(src, dst, sems.at[i]) for i, (src, dst) in enumerate(zip(srcs, dsts))
+    ]
+    for copy in copies:
+        copy.start()
+    for copy in copies:
+        copy.wait()
+
+
 def solution(mesh):
     sections, parts = mesh.shape["pipe"], mesh.shape["tensor"]
 
-    def per_device(query_heads, key_heads, value_heads, segment_ids, section_input, out_weight):
-        total_rows, inner = query_heads.shape[1:]
-        rows, features = section_input.shape[1:]
+    def per_device(*args):
+        args = [pltpu.with_memory_space_constraint(a, pltpu.HBM) for a in args]
+        total_rows, inner = args[0].shape[1:]
+        rows, features = args[4].shape[1:]
         blocks = 8
         width = features // (2 * blocks)
         ev_blocks = 8
@@ -277,30 +315,32 @@
         any_spec = pl.BlockSpec(memory_space=pl.ANY)
         vmem_spec = pl.BlockSpec(memory_space=pltpu.VMEM)
         dma = pltpu.SemaphoreType.DMA
-        return pl.pallas_call(
+        shapes = (
+            jax.ShapeDtypeStruct((1, rows, features), bf16),
+            jax.ShapeDtypeStruct((1, rows, features), bf16),
+            jax.ShapeDtypeStruct((1, rows), f32),
+        )
+        outs = pl.pallas_call(
             functools.partial(kernel, dims),
-            out_shape=(
-                jax.ShapeDtypeStruct((1, rows, features), bf16),
-                jax.ShapeDtypeStruct((1, rows, features), bf16),
-                jax.ShapeDtypeStruct((1, rows), f32),
-            ),
+            out_shape=shapes,
             in_specs=[any_spec, any_spec, any_spec, vmem_spec, any_spec, any_spec],
             out_specs=(any_spec, any_spec, vmem_spec),
             scratch_shapes=[
-                pltpu.VMEM((total_rows, inner), bf16),
+                pltpu.VMEM((2, 2 * rows, inner), bf16),
                 pltpu.VMEM((total_rows, inner), bf16),
                 pltpu.VMEM((total_rows, inner), bf16),
                 pltpu.VMEM((rows, features), bf16),
                 pltpu.VMEM((2, blocks, inner, width), bf16),
                 pltpu.VMEM((total_rows, inner), bf16),
-                pltpu.VMEM((rows, total_rows), f32),
+                pltpu.VMEM((total_rows, rows), f32),
+                pltpu.VMEM((total_rows, 2 * rows), f32),
                 pltpu.VMEM((2, blocks, 3 * rows, width), f32),
                 pltpu.VMEM((2, blocks, rows, width), bf16),
                 pltpu.VMEM((2, 3, blocks, rows, width), bf16),
                 pltpu.VMEM((ev_blocks, ev_rows, features), bf16),
                 pltpu.VMEM((rows, HD), f32),
                 pltpu.VMEM((rows, width), bf16),
-                dma((4,)),
+                dma((9,)),
                 dma((2, blocks)),
                 dma((2, 3, blocks)),
                 dma((2, 3, blocks)),
@@ -312,9 +352,17 @@
                 dma((2, blocks)),
             ],
             compiler_params=pltpu.CompilerParams(
-                collective_id=0, has_side_effects=True, vmem_limit_bytes=60 * 1024 * 1024
+                collective_id=0, has_side_effects=True, vmem_limit_bytes=47 * 1024 * 1024
             ),
-        )(query_heads, key_heads, value_heads, segment_ids, section_input, out_weight)
+        )(*args)
+        return pl.pallas_call(
+            finish,
+            out_shape=shapes,
+            in_specs=[vmem_spec] * 3,
+            out_specs=(any_spec,) * 3,
+            scratch_shapes=[dma((3,))],
+            compiler_params=pltpu.CompilerParams(vmem_limit_bytes=8 * 1024 * 1024),
+        )(*outs)
 
     return jax.shard_map(
         per_device,

time: 96.4 us -> 88.9 us (0.922)
  local copies, waits for them, and re-layouts: 5.08 us -> 0 us
  Pallas kernels: 90.5 us -> 88.1 us
    unnamed x7 -> x0, local copies, waits for them, and re-layouts: 5.08 us -> none
    pallas_call x1 -> x2, Pallas kernels: 90.5 us -> 88.1 us  [the longest x1 86.1 us: per_device(): pl.pallas_call(functools.partial(kernel, dims), out_shape=shapes, in_spec...]
where the time goes in v2:
time: 88.9 us; the launch traced here: 88.8 us
  Pallas kernels  88.1 us (99%)
    pallas_call x1, Pallas kernels, per_device(): pl.pallas_call(functools.partial(kernel, dims), out_shape=shapes, in_spec...  86.1 us
    pallas_call x1, Pallas kernels, per_device(): pl.pallas_call(finish, out_shape=shapes, in_specs=[vmem_spec] * 3, out_sp...  2.04 us

profile of v2, /device:TPU:6, one launch (start us, length us, event | category | flops | bytes accessed | tf_op | source)
XLA Modules:
  0.0 88.8 jit_solution(16534977541648605664)
XLA Ops:
  0.6 86.1 %shard_map.85 = (bf16[1,128,8192]{2,1,0:T(8,128)(2,1)S(1)}, bf16[1,128,8192]{2,1,0:T(8,128)(2,1)S(1)}, f32[1,128]{1,0:T(1,128)S(1)}) custom-call(bf16[1,512,1024]{2,1,0:T(8,128)(2,1)} %q_hbm.1, bf16[1,512,1024]{2,1,0:T(8,128)(2,1)} %k_hbm.1, bf16[1,512,1024]{2,1,0:T(8,128)(2,1)} %v_hbm.1, s32[1,512]{1,0:T(1,128)} %seg_ref.1, bf16[1,128,8192]{2,1,0:T(8,128)(2,1)} %x_hbm.1, ...), custom_call_target="tpu_custom_call" | custom-call | tf_op jit(solution)/shard_map/pallas_call | solution.py:323
  86.7 2.0 %shard_map.86 = (bf16[1,128,8192]{2,1,0:T(8,128)(2,1)}, bf16[1,128,8192]{2,1,0:T(8,128)(2,1)}, f32[1,128]{1,0:T(1,128)}) custom-call(bf16[1,128,8192]{2,1,0:T(8,128)(2,1)S(1)} %get-tuple-element.6.refs_0_, bf16[1,128,8192]{2,1,0:T(8,128)(2,1)S(1)} %get-tuple-element.7.refs_1_, f32[1,128]{1,0:T(1,128)S(1)} %get-tuple-element.8.refs_2_), custom_call_target="tpu_custom_call" | custom-call | tf_op jit(solution)/shard_map/pallas_call | solution.py:358

commit v3 on v2

--- a/solution.py
+++ b/solution.py
@@ -12,6 +12,7 @@
 NEG = -1e30
 MESH = pl.DeviceIdType.MESH
 UNROLL = 4
+CUTS = 4
 
 
 def kernel(
@@ -288,11 +289,15 @@
     lax.fori_loop(0, ev_blocks, drain_ev, 0)
 
 
-def finish(*refs):
-    srcs, dsts, sems = refs[:3], refs[3:6], refs[6]
-    copies = [
-        pltpu.make_async_copy(src, dst, sems.at[i]) for i, (src, dst) in enumerate(zip(srcs, dsts))
-    ]
+def finish(recv_ref, ev_ref, scale_ref, recv_hbm, ev_hbm, scale_hbm, sems):
+    step = recv_ref.shape[1] // CUTS
+    copies = [pltpu.make_async_copy(scale_ref, scale_hbm, sems.at[2 * CUTS])]
+    for i in range(CUTS):
+        at = pl.ds(i * step, step)
+        for n, (src, dst) in enumerate(((recv_ref, recv_hbm), (ev_ref, ev_hbm))):
+            copies.append(
+                pltpu.make_async_copy(src.at[0, at, :], dst.at[0, at, :], sems.at[2 * i + n])
+            )
     for copy in copies:
         copy.start()
     for copy in copies:
@@ -360,7 +365,7 @@
             out_shape=shapes,
             in_specs=[vmem_spec] * 3,
             out_specs=(any_spec,) * 3,
-            scratch_shapes=[dma((3,))],
+            scratch_shapes=[dma((2 * CUTS + 1,))],
             compiler_params=pltpu.CompilerParams(vmem_limit_bytes=8 * 1024 * 1024),
         )(*outs)
 

time: 88.9 us -> 89 us (level)
  no operation moved by 1% of the time
where the time goes in v3:
time: 89 us; the launch traced here: 88.8 us
  Pallas kernels  88.2 us (99%)
    pallas_call x1, Pallas kernels, per_device(): pl.pallas_call(functools.partial(kernel, dims), out_shape=shapes, in_spec...  86.1 us
    pallas_call x1, Pallas kernels, per_device(): pl.pallas_call(finish, out_shape=shapes, in_specs=[vmem_spec] * 3, out_sp...  2.08 us

profile of v3, /device:TPU:6, one launch (start us, length us, event | category | flops | bytes accessed | tf_op | source)
XLA Modules:
  0.0 88.8 jit_solution(3975653797699299169)
XLA Ops:
  0.6 86.1 %shard_map.85 = (bf16[1,128,8192]{2,1,0:T(8,128)(2,1)S(1)}, bf16[1,128,8192]{2,1,0:T(8,128)(2,1)S(1)}, f32[1,128]{1,0:T(1,128)S(1)}) custom-call(bf16[1,512,1024]{2,1,0:T(8,128)(2,1)} %q_hbm.1, bf16[1,512,1024]{2,1,0:T(8,128)(2,1)} %k_hbm.1, bf16[1,512,1024]{2,1,0:T(8,128)(2,1)} %v_hbm.1, s32[1,512]{1,0:T(1,128)} %seg_ref.1, bf16[1,128,8192]{2,1,0:T(8,128)(2,1)} %x_hbm.1, ...), custom_call_target="tpu_custom_call" | custom-call | tf_op jit(solution)/shard_map/pallas_call | solution.py:328
  86.7 2.1 %shard_map.86 = (bf16[1,128,8192]{2,1,0:T(8,128)(2,1)}, bf16[1,128,8192]{2,1,0:T(8,128)(2,1)}, f32[1,128]{1,0:T(1,128)}) custom-call(bf16[1,128,8192]{2,1,0:T(8,128)(2,1)S(1)} %get-tuple-element.6.recv_ref, bf16[1,128,8192]{2,1,0:T(8,128)(2,1)S(1)} %get-tuple-element.7.ev_ref, f32[1,128]{1,0:T(1,128)S(1)} %get-tuple-element.8.scale_ref), custom_call_target="tpu_custom_call" | custom-call | tf_op jit(solution)/shard_map/pallas_call | solution.py:363
